TPU v7x, 32 devices: a whole 2x2x4 slice. The times are simulated.
32 devices in a mesh: dp: 8 (over z, x), tensor: 4 (over y, core).
Axes of the slice: x: 2, y: 2, z: 4, core: 2. Of those that a mesh axis runs over, the one named last changes fastest.
Arguments:
- tokens: bfloat16 [512, 4096], P('dp', 'tensor')
- norm_gain: float32 [4096], P('tensor'), may hold values from 0.5 to 1.5
- eraser_mean: float32 [4096], P('tensor'), may hold values from -6 to 6
- eraser_in: float32 [4096, 128], P('tensor'), may hold values from -0.09375 to 0.09375
- eraser_out: float32 [4096, 128], P('tensor'), may hold values from -0.5 to 0.5
- router: float32 [4096, 8], P('tensor'), may hold values from -0.09375 to 0.09375
- expert_ids: int32 [512, 2], P('dp'), may hold values from 0 to 7, as said below
- slots: int32 [512, 2], P('dp'), may hold values from 0 to 63, as said below
- w_gate: bfloat16 [8, 4096, 14336], P('dp', None, 'tensor'), may hold values from -0.09375 to 0.09375
- w_up: bfloat16 [8, 4096, 14336], P('dp', None, 'tensor'), may hold values from -0.09375 to 0.09375
- w_down: bfloat16 [8, 14336, 4096], P('dp', 'tensor'), may hold values from -0.0625 to 0.0625
Outputs:
- moe_out: bfloat16 [512, 4096], P('dp', 'tensor')
Inputs may be any that keep to these rules, and one draw needn't show every extreme that they name: `expert_ids`: the two experts of a token differ. Within each aligned block of 64 tokens, the choices naming one expert have the slots 0, 1, 2, ... with no repeats; choices with a slot of 24 or more are dropped.
All inputs are finite; a program needn't handle non-finite values.
Results may differ from a plain program's by a relative error of at most 0.0065.
Values may be sent and summed in bfloat16 or wider, within the bound.
A program may use at most 128 MiB of HBM per device.

v0:
```python
import jax
import jax.numpy as jnp
from jax import lax
from jax.sharding import PartitionSpec as P

E = 8


def on_device(
    tokens,
    norm_gain,
    eraser_mean,
    eraser_in,
    eraser_out,
    router,
    expert_ids,
    slots,
    w_gate,
    w_up,
    w_down,
):
    highest = lax.Precision.HIGHEST
    part_count = lax.axis_size("dp") // E
    tok_rows = tokens.shape[0]
    capacity = 3 * tok_rows // 8
    width = tokens.shape[1] * lax.axis_size("tensor")
    values = tokens.astype(jnp.float32)
    gained = values * norm_gain[None, :]
    squares = jnp.sum(values * values, axis=1)
    gained_in = jnp.dot(gained, eraser_in, precision=highest, preferred_element_type=jnp.float32)
    mean_in = jnp.dot(
        eraser_mean[None, :], eraser_in, precision=highest, preferred_element_type=jnp.float32
    )
    router_out = jnp.dot(
        router.T, eraser_out, precision=highest, preferred_element_type=jnp.float32
    )
    routed = jnp.dot(router.T, gained.T, precision=highest, preferred_element_type=jnp.float32)
    rank = eraser_in.shape[1]
    narrow = jnp.concatenate([routed, squares[None, :]], axis=0)
    narrow = jnp.pad(narrow, ((0, 0), (0, rank - tok_rows)))
    packed = lax.psum(jnp.concatenate([gained_in, router_out, mean_in, narrow], axis=0), "tensor")
    gained_in = packed[:tok_rows]
    router_out = packed[tok_rows : tok_rows + E]
    mean_in = packed[tok_rows + E]
    routed = packed[tok_rows + E + 1 : tok_rows + 2 * E + 1, :tok_rows].T
    squares = packed[tok_rows + 2 * E + 1, :tok_rows]
    inv_rms = lax.rsqrt(squares / width + 1e-05)
    projected = inv_rms[:, None] * gained_in - mean_in[None, :]
    cleaned = inv_rms[:, None] * gained - jnp.dot(
        projected, eraser_out.T, precision=highest, preferred_element_type=jnp.float32
    )
    logits = inv_rms[:, None] * routed - jnp.dot(
        projected, router_out.T, precision=highest, preferred_element_type=jnp.float32
    )
    erased = cleaned.astype(jnp.bfloat16)
    chosen = (expert_ids[:, :, None] == jnp.arange(E, dtype=jnp.int32)[None, None, :]).astype(
        jnp.float32
    )
    picked = jnp.sum(chosen * logits[:, None, :], axis=2)
    first_gate = jax.nn.sigmoid(picked[:, 0] - picked[:, 1])
    gate_pair = jnp.stack([first_gate, 1.0 - first_gate], axis=1)
    kept_mask = slots < capacity
    target = expert_ids * capacity + slots
    columns = jnp.arange(E * capacity, dtype=jnp.int32)
    match = ((target[:, :, None] == columns[None, None, :]) & kept_mask[:, :, None]).astype(
        jnp.float32
    )
    placing = jnp.sum(match, axis=1).T.astype(jnp.bfloat16)
    weights = jnp.sum(match * gate_pair[:, :, None], axis=1)
    filled = jnp.dot(placing, erased, preferred_element_type=jnp.float32).astype(jnp.bfloat16)
    received = lax.all_to_all(
        jnp.repeat(filled.reshape(E, capacity, erased.shape[1]), part_count, axis=0),
        "dp",
        split_axis=0,
        concat_axis=0,
        tiled=True,
    )
    received = lax.all_gather(received, "tensor", axis=2, tiled=True)
    sources, count, features = received.shape
    flat_rows = received.reshape(sources * count, features)
    gate_act = jnp.dot(flat_rows, w_gate[0], preferred_element_type=jnp.float32)
    up_act = jnp.dot(flat_rows, w_up[0], preferred_element_type=jnp.float32)
    hidden = (jax.nn.silu(gate_act) * up_act).astype(jnp.bfloat16)
    outputs = (
        jnp.dot(hidden, w_down[0], preferred_element_type=jnp.float32)
        .reshape(sources, count, features)
        .astype(jnp.bfloat16)
    )
    reduced = lax.psum_scatter(outputs, "tensor", scatter_dimension=2, tiled=True)
    returned = lax.all_to_all(reduced, "dp", split_axis=0, concat_axis=0, tiled=True)
    summed = jnp.sum(
        returned.astype(jnp.float32).reshape(E, part_count, capacity, returned.shape[2]), axis=1
    ).reshape(E * capacity, returned.shape[2])
    mixed = jnp.dot(weights, summed, precision=highest, preferred_element_type=jnp.float32)
    return mixed.astype(jnp.bfloat16)


def solution(mesh):
    in_specs = (
        P("dp", "tensor"),
        P("tensor"),
        P("tensor"),
        P("tensor", None),
        P("tensor", None),
        P("tensor", None),
        P("dp", None),
        P("dp", None),
        P("dp", None, "tensor"),
        P("dp", None, "tensor"),
        P("dp", "tensor", None),
    )
    out_specs = P("dp", "tensor")
    return jax.shard_map(
        on_device, mesh=mesh, in_specs=in_specs, out_specs=out_specs, check_vma=False
    )
```

profile of v0, /device:TPU:0, one launch (start us, length us, event | category | flops | bytes accessed | tf_op | source)
XLA Modules:
  0.0 159.8 jit_solution(10361582863395513640)
XLA Ops:
  6.5 0.0 copy-start
  6.5 0.0 copy-start.3
  6.5 0.0 copy-start.2
  6.5 0.0 all-gather.2.cloned.1.call-start
  6.5 1.1 fusion.18
  7.6 1.4 fusion.36
  9.1 1.6 fusion.17
  10.6 1.2 convolution_bitcast_fusion
  11.8 0.0 copy-done
  11.8 1.2 fusion.35
  13.1 13.2 %psum.7 = f32[82,128]{1,0:T(8,128)S(1)} all-reduce(f32[82,128]{1,0:T(8,128)S(1)} %pad_maximum_fusion), channel_id=1, replica_groups=mesh['dp'=8,'tensor'=4] {'tensor'}, use_global_device_ids=true, to_apply=%region_1.2 | all-reduce | flops 10496 | bytes 83968 | tf_op jit(solution)/shard_map/psum | solution.py:41
  26.3 0.2 convolution_subtract_fusion.1
  26.5 1.6 %fusion.15 = bf16[64,1024]{1,0:T(8,128)(2,1)S(1)} fusion(f32[1024,128]{1,0:T(8,128)S(1)} %copy-done, bf16[64,1024]{1,0:T(8,128)(2,1)} %param.11, f32[64]{0:T(128)S(1)} %fusion.34, f32[1024]{0:T(1024)} %param.12, f32[82,128]{1,0:T(8,128)S(1)} %psum.7, f32[128]{0:T(128)S(1)} %slice_bitcast_fusion), kind=kOutput, calls=%fused_computation.11 | convolution fusion | flops 101007360 | bytes 824832 | tf_op jit(solution)/shard_map/dot_general | solution.py:49
  28.2 0.0 copy-done.3
  28.2 0.0 copy-done.2
  28.3 0.1 convert_reduce_fusion
  28.4 0.3 convolution_convert_fusion
  28.7 16.7 %all_to_all.10 = bf16[8,24,1024]{2,1,0:T(8,128)(2,1)} all-to-all(bf16[8,24,1024]{2,1,0:T(8,128)(2,1)S(1)} %bitcast.48), channel_id=1, replica_groups=mesh['dp'=8,'tensor'=4] {'dp'}, dimensions={0} | all-to-all | bytes 786432 | tf_op jit(solution)/shard_map/all_to_all | solution.py:71
  45.4 0.0 all-gather.2.cloned.1.call-update
  45.4 0.0 reduce-scatter.2.cloned.1.call-start
  45.5 18.7 %all-gather.2.cloned.1.call-done = bf16[8,24,4096]{2,1,0:T(8,128)(2,1)} async-done(((bf16[8,24,1024]{2,1,0:T(8,128)(2,1)}), bf16[8,24,4096]{2,1,0:T(8,128)(2,1)}) %all-gather.2.cloned.1.call-update) | async-done | bytes 1572880 | tf_op jit(solution)/shard_map/all_gather | solution.py:78
  64.2 0.0 copy-start.4
  64.2 15.9 %fusion.4 = f32[192,3584]{1,0:T(8,128)S(1)} fusion(bf16[192,4096]{1,0:T(8,128)(2,1)} %bitcast.51, bf16[1,4096,3584]{2,1,0:T(8,128)(2,1)} %param.19), kind=kOutput, calls=%fused_computation.4 | convolution fusion | flops 5637144576 | bytes 33685504 | tf_op jit(solution)/shard_map/dot_general | solution.py:81
  80.1 0.0 copy-done.4
  80.1 12.5 %fusion.9 = bf16[192,3584]{1,0:T(8,128)(2,1)S(1)} fusion(bf16[192,4096]{1,0:T(8,128)(2,1)S(1)} %bitcast.52, bf16[1,4096,3584]{2,1,0:T(8,128)(2,1)} %param.20, f32[192,3584]{1,0:T(8,128)S(1)} %fusion.4), kind=kOutput, calls=%fused_computation.7 | convolution fusion | flops 5641273344 | bytes 35061760 | tf_op jit(solution)/shard_map/dot_general | solution.py:82
  92.6 0.0 copy-start.1
  92.6 13.8 %fusion.12 = bf16[8,24,4096]{2,1,0:T(8,128)(2,1)} fusion(bf16[8,24,3584]{2,1,0:T(8,128)(2,1)S(1)} %bitcast.53, bf16[1,3584,4096]{2,1,0:T(8,128)(2,1)} %param.21), kind=kOutput, calls=%fused_computation.8 | convolution fusion | flops 5637931008 | bytes 32309248 | tf_op jit(solution)/shard_map/dot_general | solution.py:85
  106.4 0.0 reduce-scatter.2.cloned.1.call-update
  106.4 28.1 %reduce-scatter.2.cloned.1.call-done = bf16[8,24,1024]{2,1,0:T(8,128)(2,1)} async-done(((bf16[8,24,4096]{2,1,0:T(8,128)(2,1)}), bf16[8,24,1024]{2,1,0:T(8,128)(2,1)}) %reduce-scatter.2.cloned.1.call-update) | async-done | bytes 393232 | tf_op jit(solution)/shard_map/reduce_scatter | solution.py:89
  134.6 17.4 %all_to_all.11 = bf16[8,24,1024]{2,1,0:T(8,128)(2,1)S(1)} all-to-all(bf16[8,24,1024]{2,1,0:T(8,128)(2,1)} %reduce-scatter.2.cloned.1.call-done), channel_id=1, replica_groups=mesh['dp'=8,'tensor'=4] {'dp'}, dimensions={0} | all-to-all | bytes 786432 | tf_op jit(solution)/shard_map/all_to_all | solution.py:90
  152.0 1.0 convolution_convert_fusion.1
  153.0 0.0 copy-done.1
  (9 shorter events, 0.1 us)
Async XLA Ops:
  6.5 5.3 %copy-start = (f32[1024,128]{1,0:T(8,128)S(1)}, f32[1024,128]{1,0:T(8,128)}, u32[]{:S(2)}) copy-start(f32[1024,128]{1,0:T(8,128)} %param.15) | copy-start | bytes 1572868
  6.5 21.6 %copy-start.3 = (s32[64,2]{0,1:T(2,128)S(1)}, s32[64,2]{0,1:T(2,128)}, u32[]{:S(2)}) copy-start(s32[64,2]{0,1:T(2,128)} %param.18) | copy-start | bytes 1540
  6.5 21.7 %copy-start.2 = (s32[64,2]{0,1:T(2,128)S(1)}, s32[64,2]{0,1:T(2,128)}, u32[]{:S(2)}) copy-start(s32[64,2]{0,1:T(2,128)} %param.17) | copy-start | bytes 1540
  6.5 57.6 %all-gather.2.cloned.1.call-start = ((), (), s32[]{:S(2)}) async-start(), calls=%async_computation.3 | async-start | bytes 1966080 | tf_op jit(solution)/shard_map/all_gather | solution.py:78
  45.4 89.1 %reduce-scatter.2.cloned.1.call-start = ((), (), s32[]{:S(2)}) async-start(), calls=%async_computation.4 | async-start | bytes 1966080 | tf_op jit(solution)/shard_map/reduce_scatter | solution.py:89
  64.2 15.9 %copy-start.4 = (bf16[8,24,4096]{2,1,0:T(8,128)(2,1)S(1)}, bf16[8,24,4096]{2,1,0:T(8,128)(2,1)}, u32[]{:S(2)}) copy-start(bf16[8,24,4096]{2,1,0:T(8,128)(2,1)} %all-gather.2.cloned.1.call-done) | copy-start | bytes 4718596
  92.6 60.4 %copy-start.1 = (f32[1024,128]{1,0:T(8,128)S(1)}, f32[1024,128]{1,0:T(8,128)}, u32[]{:S(2)}) copy-start(f32[1024,128]{1,0:T(8,128)} %param.15) | copy-start | bytes 1572868
Sparse Core Ops, SparseCore 0:
  45.6 18.5 all-gather.1
  106.5 27.9 reduce-scatter.1
where the time goes:
time: 160 us
  matrix products  50.6 us (32%)
  blocking collectives  47.4 us (30%)
  waiting for transfers between devices  46.9 us (29%)
  between operations  13.5 us (8%)
    reduce_scatter x1, waiting for transfers between devices, on_device(): lax.psum_scatter(outputs, 'tensor', scatter_dimension=2, tiled=True)  28.1 us
    all_gather x1, waiting for transfers between devices, on_device(): received = lax.all_gather(received, 'tensor', axis=2, tiled=True)  18.7 us
    all_to_all x1, blocking collectives, on_device(): lax.all_to_all(reduced, 'dp', split_axis=0, concat_axis=0, tiled=True)  17.4 us
    all_to_all x1, blocking collectives, on_device(): lax.all_to_all(jnp.repeat(filled.reshape(E, capacity, erased.shape[1]), p...  16.7 us
    dot_general x1, matrix products, on_device(): gate_act = jnp.dot(flat_rows, w_gate[0], preferred_element_type=jnp.float32)  15.9 us
    dot_general x1, matrix products, on_device(): jnp.dot(hidden, w_down[0], preferred_element_type=jnp.float32)  13.8 us
    psum x1, blocking collectives, on_device(): lax.psum(jnp.concatenate([gained_in, router_out, mean_in, narrow], axis=0...  13.2 us
    dot_general x1, matrix products, on_device(): up_act = jnp.dot(flat_rows, w_up[0], preferred_element_type=jnp.float32)  12.5 us
  transfers between devices with their start and end apart: 2, of which 2 were waited for; matrix products, arithmetic and copies ran while one was open for 0% of the time, Pallas kernels for 0%

commit v1 on v0

--- a/solution.py
+++ b/solution.py
@@ -38,7 +38,8 @@
     rank = eraser_in.shape[1]
     narrow = jnp.concatenate([routed, squares[None, :]], axis=0)
     narrow = jnp.pad(narrow, ((0, 0), (0, rank - tok_rows)))
-    packed = lax.psum(jnp.concatenate([gained_in, router_out, mean_in, narrow], axis=0), "tensor")
+    row_data = jnp.concatenate([gained_in, router_out, mean_in, narrow], axis=0)
+    packed = jnp.sum(lax.all_gather(row_data, "tensor"), axis=0)
     gained_in = packed[:tok_rows]
     router_out = packed[tok_rows : tok_rows + E]
     mean_in = packed[tok_rows + E]

time: 160 us -> 155 us (0.969)
  blocking collectives: 47.4 us -> 42.7 us
    psum x1 -> x0, blocking collectives: 13.2 us -> none  [on_device(): lax.psum(jnp.concatenate([gained_in, router_out, mean_in, narrow], axis=0...]
    all_gather x0 -> x1, blocking collectives: none -> 6.81 us  [on_device(): packed = jnp.sum(lax.all_gather(row_data, 'tensor'), axis=0)]
    all_to_all x1, blocking collectives: 16.7 us -> 18.5 us  [on_device(): lax.all_to_all(jnp.repeat(filled.reshape(E, capacity, erased.shape[1]), p...]
where the time goes in v1:
time: 155 us
  matrix products  50.4 us (33%)
  waiting for transfers between devices  46.6 us (30%)
  blocking collectives  42.7 us (28%)
  between operations  13.5 us (9%)
    reduce_scatter x1, waiting for transfers between devices, on_device(): lax.psum_scatter(outputs, 'tensor', scatter_dimension=2, tiled=True)  28.1 us
    all_to_all x1, blocking collectives, on_device(): lax.all_to_all(jnp.repeat(filled.reshape(E, capacity, erased.shape[1]), p...  18.5 us
    all_gather x1, waiting for transfers between devices, on_device(): received = lax.all_gather(received, 'tensor', axis=2, tiled=True)  18.4 us
    all_to_all x1, blocking collectives, on_device(): lax.all_to_all(reduced, 'dp', split_axis=0, concat_axis=0, tiled=True)  17.4 us
    dot_general x1, matrix products, on_device(): gate_act = jnp.dot(flat_rows, w_gate[0], preferred_element_type=jnp.float32)  15.9 us
    dot_general x1, matrix products, on_device(): jnp.dot(hidden, w_down[0], preferred_element_type=jnp.float32)  13.8 us
    dot_general x1, matrix products, on_device(): up_act = jnp.dot(flat_rows, w_up[0], preferred_element_type=jnp.float32)  12.5 us
    all_gather x1, blocking collectives, on_device(): packed = jnp.sum(lax.all_gather(row_data, 'tensor'), axis=0)  6.81 us
  transfers between devices with their start and end apart: 2, of which 2 were waited for; matrix products, arithmetic and copies ran while one was open for 0% of the time, Pallas kernels for 0%

profile of v1, /device:TPU:0, one launch (start us, length us, event | category | flops | bytes accessed | tf_op | source)
XLA Modules:
  0.0 154.8 jit_solution(17050761935827041043)
XLA Ops:
  6.5 0.0 copy-start
  6.5 0.0 copy-start.2
  6.5 0.0 copy-start.4
  6.5 0.0 copy-start.3
  6.5 0.0 all-gather.4.cloned.1.call-start
  6.6 1.1 fusion.18
  7.7 1.4 fusion.36
  9.1 1.6 %fusion.17 = f32[64,128]{1,0:T(8,128)S(1)} fusion(f32[1024,128]{1,0:T(8,128)} %param.14, bf16[64,1024]{1,0:T(8,128)(2,1)} %param.11, f32[1024]{0:T(1024)} %param.12), kind=kOutput, calls=%fused_computation.18 | convolution fusion | flops 100794368 | bytes 692224 | tf_op jit(solution)/shard_map/dot_general | solution.py:30
  10.7 1.2 convolution_bitcast_fusion
  11.9 0.0 copy-done
  11.9 1.2 fusion.35
  13.1 6.8 %all-gather.1 = f32[4,82,128]{2,1,0:T(8,128)S(1)} all-gather(f32[1,82,128]{2,1,0:T(8,128)S(1)} %maximum_bitcast_fusion), channel_id=2, replica_groups=mesh['dp'=8,'tensor'=4] {'tensor'}, dimensions={0}, use_global_device_ids=true | all-gather | bytes 209920 | tf_op jit(solution)/shard_map/all_gather | solution.py:42
  19.9 0.2 convolution_subtract_fusion.1
  20.2 0.0 copy-done.2
  20.2 1.4 fusion.15
  21.6 0.0 copy-done.4
  21.6 0.0 copy-done.3
  21.7 0.1 convert_reduce_fusion
  21.8 0.3 convolution_convert_fusion
  22.1 18.5 %all_to_all.10 = bf16[8,24,1024]{2,1,0:T(8,128)(2,1)} all-to-all(bf16[8,24,1024]{2,1,0:T(8,128)(2,1)S(1)} %bitcast.50), channel_id=1, replica_groups=mesh['dp'=8,'tensor'=4] {'dp'}, dimensions={0} | all-to-all | bytes 786432 | tf_op jit(solution)/shard_map/all_to_all | solution.py:72
  40.6 0.0 all-gather.4.cloned.1.call-update
  40.6 0.0 reduce-scatter.2.cloned.1.call-start
  40.7 18.4 %all-gather.4.cloned.1.call-done = bf16[8,24,4096]{2,1,0:T(8,128)(2,1)} async-done(((bf16[8,24,1024]{2,1,0:T(8,128)(2,1)}), bf16[8,24,4096]{2,1,0:T(8,128)(2,1)}) %all-gather.4.cloned.1.call-update) | async-done | bytes 1572880 | tf_op jit(solution)/shard_map/all_gather | solution.py:79
  59.1 0.0 copy-start.5
  59.1 15.9 %fusion.4 = f32[192,3584]{1,0:T(8,128)S(1)} fusion(bf16[192,4096]{1,0:T(8,128)(2,1)} %bitcast.53, bf16[1,4096,3584]{2,1,0:T(8,128)(2,1)} %param.19), kind=kOutput, calls=%fused_computation.4 | convolution fusion | flops 5637144576 | bytes 33685504 | tf_op jit(solution)/shard_map/dot_general | solution.py:82
  75.0 0.0 copy-done.5
  75.0 12.5 %fusion.9 = bf16[192,3584]{1,0:T(8,128)(2,1)S(1)} fusion(bf16[192,4096]{1,0:T(8,128)(2,1)S(1)} %bitcast.54, bf16[1,4096,3584]{2,1,0:T(8,128)(2,1)} %param.20, f32[192,3584]{1,0:T(8,128)S(1)} %fusion.4), kind=kOutput, calls=%fused_computation.7 | convolution fusion | flops 5641273344 | bytes 35061760 | tf_op jit(solution)/shard_map/dot_general | solution.py:83
  87.5 0.0 copy-start.1
  87.6 13.8 %fusion.12 = bf16[8,24,4096]{2,1,0:T(8,128)(2,1)} fusion(bf16[8,24,3584]{2,1,0:T(8,128)(2,1)S(1)} %bitcast.55, bf16[1,3584,4096]{2,1,0:T(8,128)(2,1)} %param.21), kind=kOutput, calls=%fused_computation.8 | convolution fusion | flops 5637931008 | bytes 32309248 | tf_op jit(solution)/shard_map/dot_general | solution.py:86
  101.3 0.0 reduce-scatter.2.cloned.1.call-update
  101.4 28.1 %reduce-scatter.2.cloned.1.call-done = bf16[8,24,1024]{2,1,0:T(8,128)(2,1)} async-done(((bf16[8,24,4096]{2,1,0:T(8,128)(2,1)}), bf16[8,24,1024]{2,1,0:T(8,128)(2,1)}) %reduce-scatter.2.cloned.1.call-update) | async-done | bytes 393232 | tf_op jit(solution)/shard_map/reduce_scatter | solution.py:90
  129.5 17.4 %all_to_all.11 = bf16[8,24,1024]{2,1,0:T(8,128)(2,1)S(1)} all-to-all(bf16[8,24,1024]{2,1,0:T(8,128)(2,1)} %reduce-scatter.2.cloned.1.call-done), channel_id=1, replica_groups=mesh['dp'=8,'tensor'=4] {'dp'}, dimensions={0} | all-to-all | bytes 786432 | tf_op jit(solution)/shard_map/all_to_all | solution.py:91
  146.9 1.0 convolution_convert_fusion.1
  147.9 0.0 copy-done.1
  (10 shorter events, 0.1 us)
Async XLA Ops:
  6.5 5.3 %copy-start = (f32[1024,128]{1,0:T(8,128)S(1)}, f32[1024,128]{1,0:T(8,128)}, u32[]{:S(2)}) copy-start(f32[1024,128]{1,0:T(8,128)} %param.15) | copy-start | bytes 1572868
  6.5 13.6 %copy-start.2 = (bf16[64,1024]{1,0:T(8,128)(2,1)S(1)}, bf16[64,1024]{1,0:T(8,128)(2,1)}, u32[]{:S(2)}) copy-start(bf16[64,1024]{1,0:T(8,128)(2,1)} %param.11) | copy-start | bytes 393220
  6.5 15.0 %copy-start.4 = (s32[64,2]{0,1:T(2,128)S(1)}, s32[64,2]{0,1:T(2,128)}, u32[]{:S(2)}) copy-start(s32[64,2]{0,1:T(2,128)} %param.18) | copy-start | bytes 1540
  6.5 15.1 %copy-start.3 = (s32[64,2]{0,1:T(2,128)S(1)}, s32[64,2]{0,1:T(2,128)}, u32[]{:S(2)}) copy-start(s32[64,2]{0,1:T(2,128)} %param.17) | copy-start | bytes 1540
  6.5 52.6 %all-gather.4.cloned.1.call-start = ((), (), s32[]{:S(2)}) async-start(), calls=%async_computation.3 | async-start | bytes 1966080 | tf_op jit(solution)/shard_map/all_gather | solution.py:79
  40.6 88.9 %reduce-scatter.2.cloned.1.call-start = ((), (), s32[]{:S(2)}) async-start(), calls=%async_computation.4 | async-start | bytes 1966080 | tf_op jit(solution)/shard_map/reduce_scatter | solution.py:90
  59.1 15.9 %copy-start.5 = (bf16[8,24,4096]{2,1,0:T(8,128)(2,1)S(1)}, bf16[8,24,4096]{2,1,0:T(8,128)(2,1)}, u32[]{:S(2)}) copy-start(bf16[8,24,4096]{2,1,0:T(8,128)(2,1)} %all-gather.4.cloned.1.call-done) | copy-start | bytes 4718596
  87.5 60.4 %copy-start.1 = (f32[1024,128]{1,0:T(8,128)S(1)}, f32[1024,128]{1,0:T(8,128)}, u32[]{:S(2)}) copy-start(f32[1024,128]{1,0:T(8,128)} %param.15) | copy-start | bytes 1572868
Sparse Core Ops, SparseCore 0:
  40.7 18.3 all-gather.3
  101.5 27.9 reduce-scatter.1
